TPU v7x, 256 devices: a whole 4x4x8 slice. The times are simulated.
256 devices in a mesh: grp: 4 (over x_lo, core), blk: 64 (over y, z, x_hi).
Axes of the slice: x: 4 (x_hi: 2, x_lo: 2; x = x_hi * 2 + x_lo), y: 4, z: 8, core: 2. Of those that a mesh axis runs over, the one named last changes fastest.
Arguments:
- obs: bfloat16 [1572864, 256], P(('grp', 'blk')), may hold values from -6 to 6
- mask_bits: int32 [1572864, 32], P(('grp', 'blk')), may hold values from 0 to 255
- factors: bfloat16 [1572864, 256], P(('grp', 'blk')), may hold values from -0.375 to 0.375
- x_blocks: float32 [4, 256, 16384], P('grp', None, 'blk'), may hold values from -6 to 6
- first_moment: float32 [4, 256, 16384], P('grp', None, 'blk'), may hold values from -0.6 to 0.6
- second_moment: float32 [4, 256, 16384], P('grp', None, 'blk'), may hold values from 0.001 to 0.1
- ar_weights: float32 [25, 256], replicated, may hold values from -0.25 to 0.25
- stratum: int32 [1], replicated, may hold values from 0 to 63
Outputs:
- factors_next: bfloat16 [1572864, 256], P(('grp', 'blk'))
- x_next: float32 [4, 256, 16384], P('grp', None, 'blk')
- first_next: float32 [4, 256, 16384], P('grp', None, 'blk')
- second_next: float32 [4, 256, 16384], P('grp', None, 'blk')
All inputs are finite; a program needn't handle non-finite values.
Results may differ from a plain program's by a relative error of at most 0.0013.
Values sent between devices are 32-bit elements; how exact they have to be, the bound alone decides.
A program may use at most 64 MiB of HBM per device.

v0:
```python
import jax
import jax.numpy as jnp
from jax import lax
from jax.sharding import PartitionSpec as P

SHORT = 24
SEASON = 168


beta_one = 0.9
beta_two = 0.999
adam_eps = 1e-08
step_rate = 0.05
factor_rate = 0.002
data_scale = 0.25


def shifted(value, axis, steps):
    count = lax.axis_size(axis)
    pairs = [(source, (source + steps) % count) for source in range(count)]
    return lax.ppermute(value, axis, pairs)


def in_blocks(value, dim, count):
    lengths = value.shape
    parts = value.reshape(*lengths[:dim], count, lengths[dim] // count, *lengths[dim + 1 :])
    return jnp.moveaxis(parts, dim, 0)


def sum_at_owner(value, axis, dim):
    parts = in_blocks(value, dim, lax.axis_size(axis))
    arrived = lax.all_to_all(parts, axis, split_axis=0, concat_axis=0, tiled=True)
    return arrived.sum(axis=0)


def copy_for_each(value, axis):
    count = lax.axis_size(axis)
    return lax.all_to_all(
        jnp.broadcast_to(value[None], (count, *value.shape)), axis, 0, 0, tiled=True
    )


def laid_out(parts, dim):
    lengths = list(parts.shape[1:])
    lengths[dim] *= parts.shape[0]
    return jnp.moveaxis(parts, 0, dim).reshape(lengths)


def gathered_copies(value, axis, dim):
    parts = copy_for_each(value, axis)
    return laid_out(parts, dim)


def unpack_mask(bits):
    shifts = jnp.arange(8, dtype=jnp.int32)
    flags = jnp.bitwise_and(jnp.right_shift(bits[:, :, None], shifts[None, None, :]), 1)
    return flags.reshape(bits.shape[0], bits.shape[1] * 8).astype(jnp.float32)


def local_update(obs_tile, bits, factor_tile, block, first, second, halo, ar_weights):
    width = block.shape[1]
    mask = unpack_mask(bits)
    block_half = block.astype(jnp.bfloat16)
    predicted = jnp.dot(factor_tile, block_half, preferred_element_type=jnp.float32)
    error = (mask * (predicted - obs_tile.astype(jnp.float32))).astype(jnp.bfloat16)
    grad_factor = lax.dot_general(
        error, block_half, (((1,), (1,)), ((), ())), preferred_element_type=jnp.float32
    )
    grad_data = lax.dot_general(
        factor_tile, error, (((0,), (0,)), ((), ())), preferred_element_type=jnp.float32
    )
    extended = jnp.concatenate([halo, block], axis=1)
    lag_list = list(range(1, SHORT + 1)) + [SEASON]
    fitted = jnp.zeros_like(block)
    for index, lag in enumerate(lag_list):
        fitted = (
            fitted + ar_weights[index][:, None] * extended[:, SEASON - lag : SEASON - lag + width]
        )
    resid = block - fitted
    backward = jnp.zeros_like(block)
    for index, lag in enumerate(lag_list):
        later = jnp.pad(resid[:, lag:], ((0, 0), (0, lag)))
        backward = backward + ar_weights[index][:, None] * later
    gradient = data_scale * grad_data + resid - backward
    first_new = beta_one * first + (1.0 - beta_one) * gradient
    second_new = beta_two * second + (1.0 - beta_two) * gradient * gradient
    block_new = block - step_rate * first_new / (jnp.sqrt(second_new) + adam_eps)
    factor_new = (factor_tile.astype(jnp.float32) - factor_rate * grad_factor).astype(jnp.bfloat16)
    return (factor_new, block_new, first_new, second_new)


def body(obs, mask_bits, factors, x_blocks, first_moment, second_moment, ar_weights, stratum):
    cycle_count = lax.axis_size("blk")
    group_count = lax.axis_size("grp")
    position = lax.axis_index("blk")
    block_index = (position + stratum[0]) % cycle_count
    own_block = x_blocks[0]
    own_first = first_moment[0]
    own_second = second_moment[0]
    tail = own_block[:, own_block.shape[1] - SEASON :]
    halo = shifted(tail, "blk", 1)
    halo = jnp.where(block_index == 0, jnp.zeros_like(halo), halo)
    factor_new, block_new, first_new, second_new = local_update(
        obs, mask_bits, factors, own_block, own_first, own_second, halo, ar_weights
    )
    stacked = jnp.stack([block_new, first_new, second_new], axis=0)
    shares = sum_at_owner(stacked, "grp", 1)
    means = shares / group_count
    moved = shifted(means, "blk", -1)
    turned = gathered_copies(moved, "grp", 1)
    return (factor_new, turned[0][None], turned[1][None], turned[2][None])


def solution(mesh):
    placed = (
        P(("grp", "blk"), None),
        P(("grp", "blk"), None),
        P(("grp", "blk"), None),
        P("grp", None, "blk"),
        P("grp", None, "blk"),
        P("grp", None, "blk"),
        P(),
        P(),
    )
    return jax.shard_map(
        body,
        mesh=mesh,
        in_specs=placed,
        out_specs=(
            P(("grp", "blk"), None),
            P("grp", None, "blk"),
            P("grp", None, "blk"),
            P("grp", None, "blk"),
        ),
        check_vma=False,
    )
```

profile of v0, /device:TPU:1, one launch (start us, length us, event | category | flops | bytes accessed | tf_op | source)
XLA Modules:
  0.0 75.8 jit_solution(8999775872551015702)
XLA Ops:
  0.6 1.1 %slice.353 = f32[256,168]{1,0:T(8,128)S(1)} slice(f32[256,256]{1,0:T(8,128)} %bitcast.88), slice={[0:256], [88:256]} | slice | bytes 344064 | tf_op jit(solution)/shard_map/slice | solution.py:100
  1.8 3.6 %collective-permute-start = (f32[256,168]{1,0:T(8,128)S(1)}, f32[256,168]{1,0:T(8,128)S(1)}, u32[]{:S(2)}, u32[]{:S(2)}) collective-permute-start(f32[256,168]{1,0:T(8,128)S(1)} %slice.353), channel_id=1, source_target_pairs={{0,1},{1,2},{2,3},{3,4},{4,5},{5,6},{6,7},{7,8},{8,9},{9,10},{10,1... | collective-permute-start | bytes 516104 | tf_op jit(solution)/shard_map/ppermute | solution.py:21
  6.1 3.4 %broadcast_bitcast_fusion = s32[6144,256]{0,1:T(8,128)} fusion(s32[6144,32]{0,1:T(8,128)S(1)} %copy-done), kind=kLoop, calls=%fused_computation.6 | loop fusion | bytes 7077888 | tf_op jit(solution)/shard_map/shift_right_arithmetic | solution.py:56
  9.6 6.6 %copy.14 = s32[6144,256]{1,0:T(8,128)} copy(s32[6144,256]{0,1:T(8,128)} %broadcast_bitcast_fusion) | data formatting | bytes 12582912 | tf_op jit(solution)/shard_map/shift_right_arithmetic | solution.py:56
  16.3 6.1 %fusion.2 = bf16[6144,256]{1,0:T(8,128)(2,1)S(1)} fusion(bf16[6144,256]{1,0:T(8,128)(2,1)} %param.10, bf16[6144,256]{1,0:T(8,128)(2,1)} %param.8, s32[6144,256]{1,0:T(8,128)} %copy.14, s32[256]{0:T(256)S(1)} %shift_right_arithmetic.23, f32[1,256,256]{2,1,0:T(8,128)S(1)} %copy-done.3), kind=kOutput, calls=%fused_computation.4 | convolution fusion | flops 816316416 | bytes 15991808 | tf_op jit(solution)/shard_map/dot_general | solution.py:64
  22.5 4.2 %fusion.12 = f32[256,256]{1,0:T(8,128)S(1)} fusion(f32[256,256]{1,0:T(8,128)S(1)} %bitcast.89, f32[256,168]{1,0:T(8,128)S(1)} %broadcast_select_fusion, f32[256]{0:T(256)S(1)} %bitcast.143, f32[256]{0:T(256)S(1)} %bitcast.145, f32[256]{0:T(256)S(1)} %bitcast.99, f32[256]{0:T(256)S(1)} %bitcast.101, f32[256]{0:T(256)S(1)} %bitcast.103, f32[256]{0:T(256)S(1)} %bitcast.105, ...), kind=kLoop, calls=%fused_computation.66 | loop fusion | flops 4915200 | bytes 721920 | tf_op jit(solution)/shard_map/sub | solution.py:79
  26.9 0.1 slice.424
  27.2 0.1 slice.422
  27.3 0.1 slice.421
  27.6 0.1 slice.419
  27.9 0.1 slice.417
  28.0 0.1 slice.416
  28.2 0.1 slice.415
  28.3 0.1 slice.414
  28.6 0.1 slice.412
  28.7 0.1 slice.411
  28.9 0.1 slice.410
  29.1 0.1 slice.408
  29.4 0.1 slice.406
  29.6 0.1 slice.405
  29.7 0.1 slice.404
  29.8 0.1 slice.403
  30.1 0.2 copy-done.1
  30.4 2.6 %divide_subtract_fusion = (f32[256,256]{1,0:T(8,128)S(1)}, f32[256,256]{1,0:T(8,128)S(1)}, f32[256,256]{1,0:T(8,128)S(1)}) fusion(f32[1,256,256]{2,1,0:T(8,128)S(1)} %copy-done.3, f32[1,256,256]{2,1,0:T(8,128)S(1)} %copy-done.4, f32[1,256,256]{2,1,0:T(8,128)S(1)} %copy-done.5, f32[256,88]{1,0:T(8,128)S(1)} %slice.426, f32[256]{0:T(256)S(1)} %bitcast.144, ...), kind=kOutput, calls=%fused_computation.138 | convolution fusion | flops 809435136 | bytes 14226432 | tf_op jit(solution)/shard_map/dot_general | solution.py:69
  33.1 14.0 %all_to_all.10 = f32[4,3,64,256]{3,2,1,0:T(8,128)S(1)} all-to-all(f32[4,3,64,256]{3,2,1,0:T(8,128)S(1)} %maximum_bitcast_fusion), channel_id=1, replica_groups=mesh['grp'=4,'blk'=64] {'grp'}, dimensions={0} | all-to-all | bytes 1572864 | tf_op jit(solution)/shard_map/all_to_all | solution.py:32
  47.2 7.5 %collective-permute-start.1 = (f32[3,64,256]{2,1,0:T(8,128)S(1)}, f32[3,64,256]{2,1,0:T(8,128)S(1)}, u32[]{:S(2)}, u32[]{:S(2)}) collective-permute-start(f32[3,64,256]{2,1,0:T(8,128)S(1)} %broadcast_multiply_fusion), channel_id=1, source_target_pairs={{0,63},{1,0},{2,1},{3,2},{4,3},{5,4},{6,5},{7,6},{8,7},{9,8},{10,9... | collective-permute-start | bytes 589832 | tf_op jit(solution)/shard_map/ppermute | solution.py:21
  54.7 3.2 %collective-permute-done.1 = f32[3,64,256]{2,1,0:T(8,128)S(1)} collective-permute-done((f32[3,64,256]{2,1,0:T(8,128)S(1)}, f32[3,64,256]{2,1,0:T(8,128)S(1)}, u32[]{:S(2)}, u32[]{:S(2)}) %collective-permute-start.1) | collective-permute-done | bytes 196640 | tf_op jit(solution)/shard_map/ppermute | solution.py:21
  57.9 1.0 %broadcast_in_dim.5 = f32[4,3,64,256]{3,2,1,0:T(8,128)} broadcast(f32[3,64,256]{2,1,0:T(8,128)S(1)} %collective-permute-done.1), dimensions={1,2,3} | broadcast | bytes 983040 | tf_op jit(solution)/shard_map/broadcast_in_dim | solution.py:39
  58.9 5.4 %all-to-all-start.1 = ((f32[4,3,64,256]{3,2,1,0:T(8,128)}), f32[4,3,64,256]{3,2,1,0:T(8,128)S(1)}, u32[]{:S(2)}, u32[]{:S(2)}) async-start(f32[4,3,64,256]{3,2,1,0:T(8,128)} %broadcast_in_dim.5), calls=%async_computation.1 | async-start | bytes 1572864 | tf_op jit(solution)/shard_map/all_to_all | solution.py:38
  64.2 5.5 %fusion.3 = bf16[6144,256]{1,0:T(8,128)(2,1)} fusion(bf16[6144,256]{1,0:T(8,128)(2,1)} %copy-done.2, bf16[6144,256]{1,0:T(8,128)(2,1)} %param.10, f32[1,256,256]{2,1,0:T(8,128)S(1)} %copy-done.3), kind=kOutput, calls=%fused_computation.5 | convolution fusion | flops 811597824 | bytes 9699328 | tf_op jit(solution)/shard_map/dot_general | solution.py:66
  69.8 5.1 %all-to-all-done.1 = f32[4,3,64,256]{3,2,1,0:T(8,128)S(1)} async-done(((f32[4,3,64,256]{3,2,1,0:T(8,128)}), f32[4,3,64,256]{3,2,1,0:T(8,128)S(1)}, u32[]{:S(2)}, u32[]{:S(2)}) %all-to-all-start.1) | async-done | bytes 786464 | tf_op jit(solution)/shard_map/all_to_all | solution.py:38
  74.9 0.9 %fusion.89 = (f32[1,4,64,256]{3,2,0,1:T(8,128)}, f32[1,4,64,256]{3,2,0,1:T(8,128)}, f32[1,4,64,256]{3,2,0,1:T(8,128)}) fusion(f32[3,4,64,256]{3,2,0,1:T(8,128)S(1)} %bitcast.90), kind=kLoop, calls=%fused_computation.145 | loop fusion | bytes 1572864 | tf_op jit(solution)/shard_map/slice | solution.py:111
  (31 shorter events, 1.5 us)
Async XLA Ops:
  0.6 5.5 %copy-start = (s32[6144,32]{0,1:T(8,128)S(1)}, s32[6144,32]{0,1:T(8,128)}, u32[]{:S(2)}) copy-start(s32[6144,32]{0,1:T(8,128)} %param.9) | copy-start | bytes 2359300
  1.8 20.6 %collective-permute-start = (f32[256,168]{1,0:T(8,128)S(1)}, f32[256,168]{1,0:T(8,128)S(1)}, u32[]{:S(2)}, u32[]{:S(2)}) collective-permute-start(f32[256,168]{1,0:T(8,128)S(1)} %slice.353), channel_id=1, source_target_pairs={{0,1},{1,2},{2,3},{3,4},{4,5},{5,6},{6,7},{7,8},{8,9},{9,10},{10,1... | collective-permute-start | bytes 516104 | tf_op jit(solution)/shard_map/ppermute | solution.py:21
  9.6 6.7 %copy-start.6 = (f32[25,256]{1,0:T(8,128)S(1)}, f32[25,256]{1,0:T(8,128)}, u32[]{:S(2)}) copy-start(f32[25,256]{1,0:T(8,128)} %param.14) | copy-start | bytes 76804
  9.6 6.7 %copy-start.3 = (f32[1,256,256]{2,1,0:T(8,128)S(1)}, f32[1,256,256]{2,1,0:T(8,128)}, u32[]{:S(2)}) copy-start(f32[1,256,256]{2,1,0:T(8,128)} %param.11) | copy-start | bytes 786436
  22.4 7.7 %copy-start.2 = (bf16[6144,256]{1,0:T(8,128)(2,1)}, bf16[6144,256]{1,0:T(8,128)(2,1)S(1)}, u32[]{:S(2)}) copy-start(bf16[6144,256]{1,0:T(8,128)(2,1)S(1)} %fusion.2) | copy-start | bytes 9437188
  28.4 1.9 %copy-start.1 = (bf16[6144,256]{1,0:T(8,128)(2,1)S(1)}, bf16[6144,256]{1,0:T(8,128)(2,1)}, u32[]{:S(2)}) copy-start(bf16[6144,256]{1,0:T(8,128)(2,1)} %param.10) | copy-start | bytes 9437188
  28.4 1.9 %copy-start.4 = (f32[1,256,256]{2,1,0:T(8,128)S(1)}, f32[1,256,256]{2,1,0:T(8,128)}, u32[]{:S(2)}) copy-start(f32[1,256,256]{2,1,0:T(8,128)} %param.12) | copy-start | bytes 786436
  28.5 2.0 %copy-start.5 = (f32[1,256,256]{2,1,0:T(8,128)S(1)}, f32[1,256,256]{2,1,0:T(8,128)}, u32[]{:S(2)}) copy-start(f32[1,256,256]{2,1,0:T(8,128)} %param.13) | copy-start | bytes 786436
  47.2 10.8 %collective-permute-start.1 = (f32[3,64,256]{2,1,0:T(8,128)S(1)}, f32[3,64,256]{2,1,0:T(8,128)S(1)}, u32[]{:S(2)}, u32[]{:S(2)}) collective-permute-start(f32[3,64,256]{2,1,0:T(8,128)S(1)} %broadcast_multiply_fusion), channel_id=1, source_target_pairs={{0,63},{1,0},{2,1},{3,2},{4,3},{5,4},{6,5},{7,6},{8,7},{9,8},{10,9... | collective-permute-start | bytes 589832 | tf_op jit(solution)/shard_map/ppermute | solution.py:21
  58.9 16.0 %all-to-all-start.1 = ((f32[4,3,64,256]{3,2,1,0:T(8,128)}), f32[4,3,64,256]{3,2,1,0:T(8,128)S(1)}, u32[]{:S(2)}, u32[]{:S(2)}) async-start(f32[4,3,64,256]{3,2,1,0:T(8,128)} %broadcast_in_dim.5), calls=%async_computation.1 | async-start | bytes 1572864 | tf_op jit(solution)/shard_map/all_to_all | solution.py:38
where the time goes:
time: 76.1 us; the launch traced here: 75.8 us
  local copies, waits for them, and re-layouts  16.7 us (22%)
  starting transfers between devices  16.5 us (22%)
  matrix products  14.2 us (19%)
  blocking collectives  14 us (18%)
  waiting for transfers between devices  8.36 us (11%)
  other arithmetic  4.35 us (6%)
  between operations  1.67 us (2%)
    all_to_all x1, blocking collectives, sum_at_owner(): lax.all_to_all(parts, axis, split_axis=0, concat_axis=0, tiled=True)  14 us
    ppermute x2, starting transfers between devices, shifted(): return lax.ppermute(value, axis, pairs)  11.2 us
    shift_right_arithmetic x4, local copies, waits for them, and re-layouts, unpack_mask(): jnp.right_shift(bits[:, :, None], shifts[None, None, :])  10.1 us
    dot_general x1, matrix products, local_update(): jnp.dot(factor_tile, block_half, preferred_element_type=jnp.float32)  6.1 us
    dot_general x1, matrix products, local_update(): lax.dot_general(error, block_half, (((1,), (1,)), ((), ())), preferred_el...  5.52 us
    all_to_all x1, starting transfers between devices, copy_for_each(): lax.all_to_all(jnp.broadcast_to(value[None], (count, *value.shape)), axis...  5.36 us
    all_to_all x1, waiting for transfers between devices, copy_for_each(): lax.all_to_all(jnp.broadcast_to(value[None], (count, *value.shape)), axis...  5.14 us
    sub x1, other arithmetic, local_update(): resid = block - fitted  4.21 us
  transfers between devices with their start and end apart: 3, of which 2 were waited for; matrix products, arithmetic and copies ran while one was open for 29% of the time, Pallas kernels for 0%

commit v1 on v0

v1 whole, which is shorter than its diff:
```python
import functools

import jax
import jax.numpy as jnp
from jax import lax
from jax.experimental import pallas as pl
from jax.experimental.pallas import tpu as pltpu
from jax.sharding import PartitionSpec as P

SHORT = 24
SEASON = 168
LAG_LIST = tuple(range(1, SHORT + 1)) + (SEASON,)

beta_one = 0.9
beta_two = 0.999
adam_eps = 1e-08
step_rate = 0.05
factor_rate = 0.002
data_scale = 0.25

MESH = pl.DeviceIdType.MESH
ROWS = 512
CHUNKS = 4


def kernel(
    n_blk,
    obs_hbm, mask_hbm, fac_hbm, x_hbm, m_hbm, v_hbm, war_hbm, stratum_ref,
    fnew, xout,
    both, mask, err, war_ref, block, first, second, zt, art, lhs, half_t, grad_t,
    share, got_one, held_two, sent_two, got_two, sent_three,
    load_sem, mask_sem, small_sem, halo_sem, sem_one, sem_two, sem_three, sem_four, sem_five, sem_six,
):
    series = obs_hbm.shape[0]
    rank = obs_hbm.shape[1]
    width = x_hbm.shape[2]
    rows = min(ROWS, series)
    tiles = series // rows
    piece = rank // 4 // CHUNKS
    grp = lax.axis_index("grp")
    blk = lax.axis_index("blk")
    core = lax.rem(grp, 2)
    near = lax.div(grp, 2)
    partner = (near * 2 + 1 - core, blk)
    across = ((1 - near) * 2 + core, blk)
    before = lax.rem(blk + n_blk - 1, n_blk)
    after = lax.rem(blk + 1, n_blk)
    down = ((1 - near) * 2 + core, before)
    up = ((1 - near) * 2 + core, after)
    halo_to = (grp, after)
    halo_from = (grp, before)

    barrier = pltpu.get_barrier_semaphore()
    for other in (partner, across, down, up, halo_to, halo_from):
        pl.semaphore_signal(barrier, inc=1, device_id=other, device_id_type=MESH)

    small = [
        pltpu.make_async_copy(x_hbm.at[0], block, small_sem.at[0]),
        pltpu.make_async_copy(m_hbm.at[0], first, small_sem.at[1]),
        pltpu.make_async_copy(v_hbm.at[0], second, small_sem.at[2]),
        pltpu.make_async_copy(war_hbm, war_ref, small_sem.at[3]),
    ]
    small[0].start()
    mask_copy = pltpu.make_async_copy(mask_hbm, mask, mask_sem)
    mask_copy.start()

    def loads(index):
        span = pl.ds(pl.multiple_of(index * rows, rows), rows)
        return (
            pltpu.make_async_copy(fac_hbm.at[span], both.at[span, pl.ds(0, rank)], load_sem.at[0, index]),
            pltpu.make_async_copy(obs_hbm.at[span], both.at[span, pl.ds(rank, width)], load_sem.at[1, index]),
        )

    def start_loads(index, carry):
        for copy in loads(index):
            copy.start()
        return carry

    lax.fori_loop(0, tiles, start_loads, 0)
    for copy in small[1:]:
        copy.start()

    small[0].wait()
    block_t = block[...].T
    zt[pl.ds(SEASON, width), :] = block_t
    half = block_t.astype(jnp.bfloat16)
    half_t[...] = half
    lhs[:, pl.ds(0, rank)] = half
    row_id = lax.broadcasted_iota(jnp.int32, (width, width), 0)
    col_id = lax.broadcasted_iota(jnp.int32, (width, width), 1)
    lhs[:, pl.ds(rank, width)] = jnp.where(row_id == col_id, -1.0, 0.0).astype(jnp.bfloat16)
    grad_t[...] = jnp.zeros_like(grad_t)

    pl.semaphore_wait(barrier, 6)
    halo = pltpu.make_async_remote_copy(
        src_ref=zt.at[pl.ds(width, SEASON)],
        dst_ref=zt.at[pl.ds(0, SEASON)],
        send_sem=halo_sem.at[0],
        recv_sem=halo_sem.at[1],
        device_id=halo_to,
        device_id_type=MESH,
    )
    halo.start()
    mask_copy.wait()

    bit = jnp.left_shift(1, lax.broadcasted_iota(jnp.int32, (1, 8, 1), 1))

    def one_tile(index, carry):
        span = pl.ds(pl.multiple_of(index * rows, rows), rows)
        for copy in loads(index):
            copy.wait()
        part = both[span, :]
        diff = lax.dot_general(
            lhs[...], part, (((1,), (1,)), ((), ())), preferred_element_type=jnp.float32
        )
        words = mask[:, span]
        seen = jnp.bitwise_and(words[:, None, :], bit) != 0
        diff = jnp.where(seen, diff.reshape(width // 8, 8, rows), 0.0).reshape(width, rows)
        rounded = diff.astype(jnp.bfloat16)
        err[:, span] = rounded
        grad_t[...] += lax.dot_general(
            rounded, part[:, :rank], (((1,), (0,)), ((), ())), preferred_element_type=jnp.float32
        )
        return carry

    lax.fori_loop(0, tiles, one_tile, 0)

    small[3].wait()
    halo.wait_recv()
    keep = jnp.where(lax.rem(blk + stratum_ref[0], n_blk) == 0, 0.0, 1.0)
    zt[pl.ds(0, SEASON), :] = zt[pl.ds(0, SEASON), :] * keep
    step = 64
    for start in range(0, width, step):
        fitted = jnp.zeros((step, rank), jnp.float32)
        for index, lag in enumerate(LAG_LIST):
            fitted = fitted + war_ref[pl.ds(index, 1), :] * zt[pl.ds(SEASON + start - lag, step), :]
        art[pl.ds(start, step), :] = zt[pl.ds(SEASON + start, step), :] - fitted
    art[pl.ds(width, SEASON), :] = jnp.zeros((SEASON, rank), jnp.float32)
    for start in range(0, width, step):
        backward = jnp.zeros((step, rank), jnp.float32)
        for index, lag in enumerate(LAG_LIST):
            if start + lag < width:
                backward = backward + war_ref[pl.ds(index, 1), :] * art[pl.ds(start + lag, step), :]
        spot = pl.ds(start, step)
        grad_t[spot, :] = data_scale * grad_t[spot, :] + art[spot, :] - backward

    small[1].wait()
    small[2].wait()
    gradient = grad_t[...].T
    first_new = beta_one * first[...] + (1.0 - beta_one) * gradient
    second_new = beta_two * second[...] + (1.0 - beta_two) * gradient * gradient
    block_new = block[...] - step_rate * first_new / (jnp.sqrt(second_new) + adam_eps)
    shape = (2, 2, rank // 4, width)
    share[0] = block_new.reshape(shape)
    share[1] = first_new.reshape(shape)
    share[2] = second_new.reshape(shape)

    def factors_tile(index):
        span = pl.ds(pl.multiple_of(index * rows, rows), rows)
        grad = lax.dot_general(
            err[:, span], half_t[...], (((0,), (0,)), ((), ())), preferred_element_type=jnp.float32
        )
        old = both[span, pl.ds(0, rank)].astype(jnp.float32)
        fnew[span, :] = (old - factor_rate * grad).astype(jnp.bfloat16)

    def factors_span(low, high):
        def one(index, carry):
            factors_tile(index)
            return carry

        lax.fori_loop(low, high, one, 0)

    def spot(k):
        return pl.ds(k * piece, piece)

    def remote(src, dst, sem, k, to):
        return pltpu.make_async_remote_copy(
            src_ref=src, dst_ref=dst, send_sem=sem.at[0, k], recv_sem=sem.at[1, k],
            device_id=to, device_id_type=MESH,
        )

    hop_one = [remote(share.at[:, 1 - core, :, spot(k)], got_one.at[k], sem_one, k, partner) for k in range(CHUNKS)]
    hop_two = [remote(sent_two.at[k], got_two.at[k], sem_two, k, across) for k in range(CHUNKS)]
    hop_three = [
        remote(sent_three.at[k], xout.at[:, core, near, spot(k)], sem_three, k, down) for k in range(CHUNKS)
    ]
    landed = [xout.at[:, core, 1 - near, spot(k)] for k in range(CHUNKS)]
    hop_four = [remote(landed[k], landed[k], sem_four, k, across) for k in range(CHUNKS)]
    hop_five = [remote(landed[k], landed[k], sem_five, k, partner) for k in range(CHUNKS)]
    crossed = [xout.at[:, core, near, spot(k)] for k in range(CHUNKS)]
    hop_six = [remote(crossed[k], crossed[k], sem_six, k, partner) for k in range(CHUNKS)]

    cuts = [tiles * i // 3 for i in range(4)]
    for k in range(CHUNKS):
        hop_one[k].start()
    factors_span(cuts[0], cuts[1])
    for k in range(CHUNKS):
        hop_one[k].wait_recv()
        sent_two[k] = share[:, core, 1 - near, spot(k)] + got_one[k, :, 1 - near]
        held_two[k] = share[:, core, near, spot(k)] + got_one[k, :, near]
        hop_two[k].start()
    factors_span(cuts[1], cuts[2])
    for k in range(CHUNKS):
        hop_two[k].wait_recv()
        sent_three[k] = (held_two[k] + got_two[k]) * 0.25
        hop_three[k].start()
    factors_span(cuts[2], cuts[3])
    for k in range(CHUNKS):
        hop_three[k].wait_recv()
        hop_four[k].start()
        hop_five[k].start()
    for k in range(CHUNKS):
        hop_four[k].wait_recv()
        hop_six[k].start()
    for k in range(CHUNKS):
        hop_five[k].wait_recv()
        hop_six[k].wait_recv()
    halo.wait_send()
    for hop in (hop_one, hop_two, hop_three, hop_four, hop_five, hop_six):
        for k in range(CHUNKS):
            hop[k].wait_send()


def body(obs, mask_bits, factors, x_blocks, first_moment, second_moment, ar_weights, stratum):
    series, rank = factors.shape
    width = obs.shape[1]
    words = mask_bits.shape[1]
    rows = min(ROWS, series)
    tiles = series // rows
    piece = rank // 4 // CHUNKS
    n_blk = lax.axis_size("blk")
    in_hbm = pl.BlockSpec(memory_space=pltpu.HBM)
    in_vmem = pl.BlockSpec(memory_space=pltpu.VMEM)
    f32, bf16 = jnp.float32, jnp.bfloat16
    dma = pltpu.SemaphoreType.DMA
    factor_new, turned = pl.pallas_call(
        functools.partial(kernel, n_blk),
        out_shape=(
            jax.ShapeDtypeStruct((series, rank), bf16),
            jax.ShapeDtypeStruct((3, 2, 2, rank // 4, width), f32),
        ),
        in_specs=[in_hbm] * 7 + [pl.BlockSpec(memory_space=pltpu.SMEM)],
        out_specs=(in_vmem, in_vmem),
        scratch_shapes=[
            pltpu.VMEM((series, rank + width), bf16),
            pltpu.VMEM((words, series), jnp.int32),
            pltpu.VMEM((width, series), bf16),
            pltpu.VMEM((len(LAG_LIST), rank), f32),
            pltpu.VMEM((rank, width), f32),
            pltpu.VMEM((rank, width), f32),
            pltpu.VMEM((rank, width), f32),
            pltpu.VMEM((SEASON + width, rank), f32),
            pltpu.VMEM((width + SEASON, rank), f32),
            pltpu.VMEM((width, rank + width), bf16),
            pltpu.VMEM((width, rank), bf16),
            pltpu.VMEM((width, rank), f32),
            pltpu.VMEM((3, 2, 2, rank // 4, width), f32),
            pltpu.VMEM((CHUNKS, 3, 2, piece, width), f32),
            pltpu.VMEM((CHUNKS, 3, piece, width), f32),
            pltpu.VMEM((CHUNKS, 3, piece, width), f32),
            pltpu.VMEM((CHUNKS, 3, piece, width), f32),
            pltpu.VMEM((CHUNKS, 3, piece, width), f32),
            dma((2, tiles)),
            dma,
            dma((4,)),
            dma((2,)),
        ]
        + [dma((2, CHUNKS))] * 6,
        compiler_params=pltpu.CompilerParams(
            collective_id=0, has_side_effects=True, vmem_limit_bytes=48 * 1024 * 1024
        ),
        name="stratum_step",
    )(
        *[
            pltpu.with_memory_space_constraint(value, pltpu.HBM)
            for value in (obs, mask_bits.T, factors, x_blocks, first_moment, second_moment, ar_weights)
        ],
        stratum,
    )
    turned = turned.reshape(3, 1, rank, width)
    return (factor_new, turned[0], turned[1], turned[2])


def solution(mesh):
    placed = (
        P(("grp", "blk"), None),
        P(("grp", "blk"), None),
        P(("grp", "blk"), None),
        P("grp", None, "blk"),
        P("grp", None, "blk"),
        P("grp", None, "blk"),
        P(),
        P(),
    )
    return jax.shard_map(
        body,
        mesh=mesh,
        in_specs=placed,
        out_specs=(
            P(("grp", "blk"), None),
            P("grp", None, "blk"),
            P("grp", None, "blk"),
            P("grp", None, "blk"),
        ),
        check_vma=False,
    )
```

time: 76.1 us -> 40.4 us (0.53)
  Pallas kernels: 0 us -> 36.4 us
  starting transfers between devices: 16.5 us -> 0 us
  matrix products: 14.2 us -> 0 us
  local copies, waits for them, and re-layouts: 16.7 us -> 2.56 us
  blocking collectives: 14 us -> 0 us
  waiting for transfers between devices: 8.36 us -> 0 us
  other arithmetic: 4.35 us -> 0 us
    pallas_call x0 -> x1, Pallas kernels: none -> 36.4 us  [body(): pl.pallas_call(functools.partial(kernel, n_blk), out_shape=(jax.ShapeDtyp...]
    dot_general x3 -> x0, matrix products: 14.2 us -> none  [the longest x1 6.1 us: local_update(): jnp.dot(factor_tile, block_half, preferred_element_type=jnp.float32)]
    all_to_all x1 -> x0, blocking collectives: 14 us -> none  [sum_at_owner(): lax.all_to_all(parts, axis, split_axis=0, concat_axis=0, tiled=True)]
    ppermute x2 -> x0, starting transfers between devices: 11.2 us -> none  [shifted(): return lax.ppermute(value, axis, pairs)]
    shift_right_arithmetic x4 -> x0, local copies, waits for them, and re-layouts: 10.1 us -> none  [unpack_mask(): jnp.right_shift(bits[:, :, None], shifts[None, None, :])]
    all_to_all x1 -> x0, starting transfers between devices: 5.36 us -> none  [copy_for_each(): lax.all_to_all(jnp.broadcast_to(value[None], (count, *value.shape)), axis...]
    all_to_all x1 -> x0, waiting for transfers between devices: 5.14 us -> none  [copy_for_each(): lax.all_to_all(jnp.broadcast_to(value[None], (count, *value.shape)), axis...]
    slice x29 -> x1, local copies, waits for them, and re-layouts: 5.26 us -> 0.89 us  [body(): return (factor_new, turned[0], turned[1], turned[2])]
  transfers between devices with their start and end apart: 3 -> 0, of which waited for: 2 -> 0; matrix products, arithmetic and copies ran while one was open for 29% -> 0% of each run, Pallas kernels for 0% -> 0%
where the time goes in v1:
time: 40.4 us; the launch traced here: 40.3 us
  Pallas kernels  36.4 us (90%)
  local copies, waits for them, and re-layouts  2.56 us (6%)
  between operations  1.29 us (3%)
    pallas_call x1, Pallas kernels, body(): pl.pallas_call(functools.partial(kernel, n_blk), out_shape=(jax.ShapeDtyp...  36.4 us
    unnamed x1, local copies, waits for them, and re-layouts  1.66 us
    slice x1, local copies, waits for them, and re-layouts, body(): return (factor_new, turned[0], turned[1], turned[2])  0.89 us

profile of v1, /device:TPU:1, one launch (start us, length us, event | category | flops | bytes accessed | tf_op | source)
XLA Modules:
  0.0 40.3 jit_solution(14156543904880391147)
XLA Ops:
  1.3 36.4 %stratum_step.1 = (bf16[6144,256]{1,0:T(8,128)(2,1)S(1)}, f32[3,2,2,64,256]{4,3,2,1,0:T(8,128)S(1)}) custom-call(bf16[6144,256]{1,0:T(8,128)(2,1)} %obs_hbm.1, s32[32,6144]{1,0:T(8,128)} %bitcast.4, bf16[6144,256]{1,0:T(8,128)(2,1)} %fac_hbm.1, f32[1,256,256]{2,1,0:T(8,128)} %x_hbm.1, f32[1,256,256]{2,1,0:T(8,128)} %m_hbm.1, f32[1,256,256]{2,1,0:T(8,128)} %v_hbm.1, ...), custom_call_target="tpu_custom_call" | custom-call | tf_op jit(solution)/shard_map/stratum_step/pallas_call | solution.py:236
  37.7 0.9 %fusion = (f32[1,2,2,64,256]{4,3,2,1,0:T(8,128)}, f32[1,2,2,64,256]{4,3,2,1,0:T(8,128)}, f32[1,2,2,64,256]{4,3,2,1,0:T(8,128)}) fusion(f32[3,2,2,64,256]{4,3,2,1,0:T(8,128)S(1)} %get-tuple-element.7), kind=kLoop, calls=%fused_computation | loop fusion | bytes 1572864 | tf_op jit(solution)/shard_map/slice | solution.py:281
  38.6 1.7 %copy.14 = bf16[6144,256]{1,0:T(8,128)(2,1)} copy(bf16[6144,256]{1,0:T(8,128)(2,1)S(1)} %get-tuple-element.15) | data formatting | bytes 6291456

commit v2 on v0

v2 whole, which is shorter than its diff:
```python
import functools

import jax
import jax.numpy as jnp
from jax import lax
from jax.experimental import pallas as pl
from jax.experimental.pallas import tpu as pltpu
from jax.sharding import PartitionSpec as P

SHORT = 24
SEASON = 168
LAGS = SHORT + 1

beta_one = 0.9
beta_two = 0.999
adam_eps = 1e-08
step_rate = 0.05
factor_rate = 0.002
data_scale = 0.25

MESH = pl.DeviceIdType.MESH
TILES = ((0, 1024), (1024, 1536), (2560, 1536), (4096, 2048))
SIDE = ((128, 40), (0, 40))
AHEAD = ((40, 48), (88, 40))
HALF = 128
PARTS = 2
BLOCK = 64
STORES = 8


def kernel(
    n_blk,
    obs_hbm, mask_hbm, fac_hbm, x_hbm, m_hbm, v_hbm, war_hbm, stratum,
    fnew, xout,
    obs, mask, fac, err, war, block, first, second, zt, art, pt, half_t, grad,
    side_stop, ahead_stop, share, got_one, held_two, sent_two, got_two, sent_three,
    load_sem, small_sem, side_sem, ahead_sem, sem_one, sem_two, sem_three, sem_four, sem_five, sem_six,
):
    rank = obs_hbm.shape[1]
    width = x_hbm.shape[2]
    quarter = rank // 4
    piece = quarter // PARTS
    grp = lax.axis_index("grp")
    blk = lax.axis_index("blk")
    core = lax.rem(grp, 2)
    near = lax.div(grp, 2)
    far = 1 - near
    partner = (near * 2 + 1 - core, blk)
    across = (far * 2 + core, blk)
    down = (far * 2 + core, lax.rem(blk + n_blk - 1, n_blk))
    up = (far * 2 + core, lax.rem(blk + 1, n_blk))

    small = [
        pltpu.make_async_copy(x_hbm.at[0], block, small_sem.at[0]),
        pltpu.make_async_copy(war_hbm, war, small_sem.at[1]),
        pltpu.make_async_copy(m_hbm.at[0], first, small_sem.at[2]),
        pltpu.make_async_copy(v_hbm.at[0], second, small_sem.at[3]),
    ]
    small[0].start()
    loads = []
    for index, (low, rows) in enumerate(TILES):
        span = pl.ds(low, rows)
        loads.append(
            [
                pltpu.make_async_copy(fac_hbm.at[span], fac.at[span], load_sem.at[0, index]),
                pltpu.make_async_copy(mask_hbm.at[:, span], mask.at[:, span], load_sem.at[1, index]),
                pltpu.make_async_copy(obs_hbm.at[span], obs.at[span], load_sem.at[2, index]),
            ]
        )
    for copy in loads[0]:
        copy.start()

    barrier = pltpu.get_barrier_semaphore()
    for other in (partner, across, down):
        pl.semaphore_signal(barrier, inc=1, device_id=other, device_id_type=MESH)
    for copies in loads[1:]:
        for copy in copies:
            copy.start()
    for copy in small[1:]:
        copy.start()

    small[0].wait()
    block_t = block[...].T
    zt[pl.ds(SEASON, width), :] = block_t
    half = block[...].astype(jnp.bfloat16)
    half_t[...] = block_t.astype(jnp.bfloat16)
    grad[...] = jnp.zeros_like(grad)
    art[pl.ds(width, BLOCK), :] = jnp.zeros((BLOCK, rank), jnp.float32)
    spread_row = lax.broadcasted_iota(jnp.int32, (width // 8, width), 0)
    spread_col = lax.broadcasted_iota(jnp.int32, (width // 8, width), 1)
    spread = jnp.where(jnp.right_shift(spread_col, 3) == spread_row, 1.0, 0.0).astype(jnp.bfloat16)
    bit = jnp.left_shift(1, jnp.bitwise_and(lax.broadcasted_iota(jnp.int32, (1, width), 1), 7))

    def remote(src, dst, sem, k, to):
        return pltpu.make_async_remote_copy(
            src_ref=src, dst_ref=dst, send_sem=sem.at[0, k], recv_sem=sem.at[1, k],
            device_id=to, device_id_type=MESH,
        )

    side_one, side_two, ahead_one, ahead_two = [], [], [], []
    for k, (low, rows) in enumerate(SIDE):
        stop = side_stop.at[k, pl.ds(0, rows)]
        side_one.append(remote(zt.at[pl.ds(width + low, rows)], stop, side_sem, k, across))
        side_two.append(remote(stop, zt.at[pl.ds(low, rows)], side_sem, 2 + k, up))
    for k, (low, rows) in enumerate(AHEAD):
        stop = ahead_stop.at[k, pl.ds(0, rows)]
        ahead_one.append(remote(zt.at[pl.ds(width + low, rows)], stop, ahead_sem, k, up))
        ahead_two.append(remote(stop, zt.at[pl.ds(low, rows)], ahead_sem, 2 + k, across))

    pl.semaphore_wait(barrier, 3)
    for k in range(2):
        side_one[k].start()
        ahead_one[k].start()

    def error_tile(index):
        low, rows = TILES[index]
        span = pl.ds(low, rows)
        for copy in loads[index]:
            copy.wait()
        part = fac[span, :]
        diff = jnp.dot(part, half, preferred_element_type=jnp.float32) - obs[span, :].astype(jnp.float32)
        words = mask[:, span].astype(jnp.float32).astype(jnp.bfloat16)
        wide = lax.dot_general(words, spread, (((0,), (0,)), ((), ())), preferred_element_type=jnp.float32)
        seen = jnp.bitwise_and(wide.astype(jnp.int32), bit) != 0
        rounded = jnp.where(seen, diff, 0.0).astype(jnp.bfloat16)
        err[span, :] = rounded
        grad[...] += lax.dot_general(
            part, rounded, (((0,), (0,)), ((), ())), preferred_element_type=jnp.float32
        )

    def factors_span(low, rows):
        span = pl.ds(low, rows)
        step = jnp.dot(err[span, :], half_t[...], preferred_element_type=jnp.float32)
        fnew[span, :] = (fac[span, :].astype(jnp.float32) - factor_rate * step).astype(jnp.bfloat16)

    def weight(lag_index, lanes):
        return war[pl.ds(lag_index, 1), lanes]

    def residual(start, lanes):
        near_rows = zt[pl.ds(SEASON - SHORT + start, BLOCK + SHORT), lanes]
        fitted = weight(SHORT, lanes) * zt[pl.ds(start, BLOCK), lanes]
        for turn in range(8):
            moved = near_rows if turn == 0 else pltpu.roll(near_rows, turn, 0)
            for tile in range(4):
                lag = 8 * tile + turn
                if 1 <= lag <= SHORT:
                    low = SHORT - 8 * tile
                    fitted = fitted + weight(lag - 1, lanes) * moved[low : low + BLOCK]
        art[pl.ds(start, BLOCK), lanes] = near_rows[SHORT:] - fitted

    def prior_gradient(start, lanes):
        rows = art[pl.ds(start, BLOCK + SHORT), lanes]
        total = rows[:BLOCK]
        for turn in range(8):
            moved = rows if turn == 0 else pltpu.roll(rows, BLOCK + SHORT - turn, 0)
            for tile in range(4):
                lag = 8 * tile + turn
                if 1 <= lag <= SHORT:
                    total = total - weight(lag - 1, lanes) * moved[8 * tile : 8 * tile + BLOCK]
        if start + SEASON < width:
            total = total - weight(SHORT, lanes) * art[pl.ds(start + SEASON, BLOCK), lanes]
        pt[pl.ds(start, BLOCK), lanes] = total

    all_lanes = [pl.ds(at, 128) for at in range(0, rank, 128)]

    def update(which):
        starts = [which * HALF + at for at in range(0, HALF, BLOCK)]
        for start in starts:
            for lanes in all_lanes:
                residual(start, lanes)
        for start in starts:
            for lanes in all_lanes:
                prior_gradient(start, lanes)
        cols = pl.ds(which * HALF, HALF)
        gradient = data_scale * grad[:, cols] + pt[cols, :].T
        first_new = beta_one * first[:, cols] + (1.0 - beta_one) * gradient
        second_new = beta_two * second[:, cols] + (1.0 - beta_two) * gradient * gradient
        block_new = block[:, cols] - step_rate * first_new / (jnp.sqrt(second_new) + adam_eps)
        shape = (2, 2, quarter, HALF)
        share[which, 0] = block_new.reshape(shape)
        share[which, 1] = first_new.reshape(shape)
        share[which, 2] = second_new.reshape(shape)

    chunks = [(which, pl.ds(p * piece, piece)) for which in (1, 0) for p in range(PARTS)]
    hop_one, hop_two, hop_three, hop_four, hop_five, hop_six = [], [], [], [], [], []
    for k, (which, ranks) in enumerate(chunks):
        landed = xout.at[which, :, core, far, ranks]
        crossed = xout.at[which, :, core, near, ranks]
        hop_one.append(remote(share.at[which, :, 1 - core, :, ranks], got_one.at[k], sem_one, k, partner))
        hop_two.append(remote(sent_two.at[k], got_two.at[k], sem_two, k, across))
        hop_three.append(remote(sent_three.at[k], crossed, sem_three, k, down))
        hop_four.append(remote(landed, landed, sem_four, k, across))
        hop_five.append(remote(landed, landed, sem_five, k, partner))
        hop_six.append(remote(crossed, crossed, sem_six, k, partner))

    def fold_core(k):
        which, ranks = chunks[k]
        hop_one[k].wait_recv()
        sent_two[k] = share[which, :, core, far, ranks] + got_one[k, :, far]
        hop_two[k].start()
        held_two[k] = share[which, :, core, near, ranks] + got_one[k, :, near]

    def fold_chip(k):
        hop_two[k].wait_recv()
        sent_three[k] = (held_two[k] + got_two[k]) * 0.25
        hop_three[k].start()

    def spread_landed(k):
        hop_three[k].wait_recv()
        hop_four[k].start()
        hop_five[k].start()

    def spread_crossed(k):
        hop_four[k].wait_recv()
        hop_six[k].start()

    error_tile(0)
    error_tile(1)
    for k in range(2):
        side_one[k].wait_recv()
        side_two[k].start()
    error_tile(2)
    error_tile(3)
    for k in range(2):
        ahead_one[k].wait_recv()
        ahead_two[k].start()

    for copy in small[1:]:
        copy.wait()
    keep = jnp.where(lax.rem(blk + stratum[0], n_blk) == 0, 0.0, 1.0)
    side_two[0].wait_recv()
    late = pl.ds(SIDE[0][0], SIDE[0][1])
    zt[late, :] = zt[late, :] * keep
    update(1)
    hop_one[0].start()
    hop_one[1].start()
    factors_span(0, 1024)
    fold_core(0)
    fold_core(1)
    side_two[1].wait_recv()
    for k in range(2):
        ahead_two[k].wait_recv()
    early = pl.ds(0, SIDE[0][0])
    zt[early, :] = zt[early, :] * keep
    update(0)
    hop_one[2].start()
    hop_one[3].start()
    factors_span(1024, 1024)
    fold_core(2)
    fold_core(3)
    fold_chip(0)
    fold_chip(1)
    factors_span(2048, 2048)
    fold_chip(2)
    spread_landed(0)
    fold_chip(3)
    spread_landed(1)
    factors_span(4096, 2048)
    spread_landed(2)
    spread_crossed(0)
    spread_landed(3)
    spread_crossed(1)
    spread_crossed(2)
    spread_crossed(3)
    for k in range(2 * PARTS):
        hop_five[k].wait_recv()
        hop_six[k].wait_recv()
    for copies in (side_one, side_two, ahead_one, ahead_two):
        for copy in copies:
            copy.wait_send()
    for hop in (hop_one, hop_two, hop_three, hop_four, hop_five, hop_six):
        for copy in hop:
            copy.wait_send()


def store_kernel(fnew, xout, fac_out, x_out, m_out, v_out, sem):
    width = x_out.shape[2]
    copies = []
    step = fnew.shape[0] // STORES
    for index in range(STORES):
        span = pl.ds(index * step, step)
        copies.append(pltpu.make_async_copy(fnew.at[span], fac_out.at[span], sem.at[index]))
    for index, out in enumerate((x_out, m_out, v_out)):
        for which in range(width // HALF):
            copies.append(
                pltpu.make_async_copy(
                    xout.at[which, index], out.at[0, :, pl.ds(which * HALF, HALF)], sem.at[STORES + 2 * index + which]
                )
            )
    for copy in copies:
        copy.start()
    for copy in copies:
        copy.wait()


def body(obs, mask_bits, factors, x_blocks, first_moment, second_moment, ar_weights, stratum):
    series, rank = factors.shape
    width = obs.shape[1]
    words = mask_bits.shape[1]
    quarter = rank // 4
    piece = quarter // PARTS
    chunks = 2 * PARTS
    n_blk = lax.axis_size("blk")
    in_hbm = pl.BlockSpec(memory_space=pltpu.HBM)
    in_vmem = pl.BlockSpec(memory_space=pltpu.VMEM)
    f32, bf16 = jnp.float32, jnp.bfloat16
    dma = pltpu.SemaphoreType.DMA
    factor_new, turned = pl.pallas_call(
        functools.partial(kernel, n_blk),
        out_shape=(
            jax.ShapeDtypeStruct((series, rank), bf16),
            jax.ShapeDtypeStruct((2, 3, 2, 2, quarter, HALF), f32),
        ),
        in_specs=[in_hbm] * 7 + [pl.BlockSpec(memory_space=pltpu.SMEM)],
        out_specs=(in_vmem, in_vmem),
        scratch_shapes=[
            pltpu.VMEM((series, width), bf16),
            pltpu.VMEM((words, series), jnp.int32),
            pltpu.VMEM((series, rank), bf16),
            pltpu.VMEM((series, width), bf16),
            pltpu.VMEM((LAGS, rank), f32),
            pltpu.VMEM((rank, width), f32),
            pltpu.VMEM((rank, width), f32),
            pltpu.VMEM((rank, width), f32),
            pltpu.VMEM((SEASON + width, rank), f32),
            pltpu.VMEM((width + BLOCK, rank), f32),
            pltpu.VMEM((width, rank), f32),
            pltpu.VMEM((width, rank), bf16),
            pltpu.VMEM((rank, width), f32),
            pltpu.VMEM((2, 48, rank), f32),
            pltpu.VMEM((2, 48, rank), f32),
            pltpu.VMEM((2, 3, 2, 2, quarter, HALF), f32),
            pltpu.VMEM((chunks, 3, 2, piece, HALF), f32),
            pltpu.VMEM((chunks, 3, piece, HALF), f32),
            pltpu.VMEM((chunks, 3, piece, HALF), f32),
            pltpu.VMEM((chunks, 3, piece, HALF), f32),
            pltpu.VMEM((chunks, 3, piece, HALF), f32),
            dma((3, len(TILES))),
            dma((4,)),
            dma((2, 4)),
            dma((2, 4)),
        ]
        + [dma((2, chunks))] * 6,
        compiler_params=pltpu.CompilerParams(
            collective_id=0, has_side_effects=True, vmem_limit_bytes=48 * 1024 * 1024
        ),
        name="stratum_step",
    )(
        *[
            pltpu.with_memory_space_constraint(value, pltpu.HBM)
            for value in (obs, mask_bits.T, factors, x_blocks, first_moment, second_moment, ar_weights)
        ],
        stratum,
    )
    turned = turned.reshape(2, 3, rank, HALF)
    return STORE(factor_new, turned, series, rank, width)


def store_plain(factor_new, turned, series, rank, width):
    whole = jnp.concatenate([turned[0], turned[1]], axis=2)
    return (factor_new, whole[0][None], whole[1][None], whole[2][None])


def store_by_kernel(factor_new, turned, series, rank, width):
    f32, bf16 = jnp.float32, jnp.bfloat16
    in_vmem = pl.BlockSpec(memory_space=pltpu.VMEM)
    in_hbm = pl.BlockSpec(memory_space=pltpu.HBM)
    out = jax.ShapeDtypeStruct((1, rank, width), f32)
    return tuple(
        pl.pallas_call(
            store_kernel,
            out_shape=(jax.ShapeDtypeStruct((series, rank), bf16), out, out, out),
            in_specs=[in_vmem] * 2,
            out_specs=[in_hbm] * 4,
            scratch_shapes=[pltpu.SemaphoreType.DMA((STORES + 6,))],
            compiler_params=pltpu.CompilerParams(vmem_limit_bytes=8 * 1024 * 1024),
            name="store_outputs",
        )(factor_new, turned)
    )


STORE = store_by_kernel


def solution(mesh):
    placed = (
        P(("grp", "blk"), None),
        P(("grp", "blk"), None),
        P(("grp", "blk"), None),
        P("grp", None, "blk"),
        P("grp", None, "blk"),
        P("grp", None, "blk"),
        P(),
        P(),
    )
    return jax.shard_map(
        body,
        mesh=mesh,
        in_specs=placed,
        out_specs=(
            P(("grp", "blk"), None),
            P("grp", None, "blk"),
            P("grp", None, "blk"),
            P("grp", None, "blk"),
        ),
        check_vma=False,
    )
```

time: 76.1 us -> 36.4 us (0.48)
  Pallas kernels: 0 us -> 35 us
  local copies, waits for them, and re-layouts: 16.7 us -> 0 us
  starting transfers between devices: 16.5 us -> 0 us
  matrix products: 14.2 us -> 0 us
  blocking collectives: 14 us -> 0 us
  waiting for transfers between devices: 8.36 us -> 0 us
  other arithmetic: 4.35 us -> 0 us
    pallas_call x0 -> x2, Pallas kernels: none -> 35 us  [the longest x1 33 us: body(): pl.pallas_call(functools.partial(kernel, n_blk), out_shape=(jax.ShapeDtyp...]
    dot_general x3 -> x0, matrix products: 14.2 us -> none  [the longest x1 6.1 us: local_update(): jnp.dot(factor_tile, block_half, preferred_element_type=jnp.float32)]
    all_to_all x1 -> x0, blocking collectives: 14 us -> none  [sum_at_owner(): lax.all_to_all(parts, axis, split_axis=0, concat_axis=0, tiled=True)]
    ppermute x2 -> x0, starting transfers between devices: 11.2 us -> none  [shifted(): return lax.ppermute(value, axis, pairs)]
    shift_right_arithmetic x4 -> x0, local copies, waits for them, and re-layouts: 10.1 us -> none  [unpack_mask(): jnp.right_shift(bits[:, :, None], shifts[None, None, :])]
    all_to_all x1 -> x0, starting transfers between devices: 5.36 us -> none  [copy_for_each(): lax.all_to_all(jnp.broadcast_to(value[None], (count, *value.shape)), axis...]
    slice x29 -> x0, local copies, waits for them, and re-layouts: 5.26 us -> none  [the longest x25 3.19 us: local_update(): later = jnp.pad(resid[:, lag:], ((0, 0), (0, lag)))]
    all_to_all x1 -> x0, waiting for transfers between devices: 5.14 us -> none  [copy_for_each(): lax.all_to_all(jnp.broadcast_to(value[None], (count, *value.shape)), axis...]
  transfers between devices with their start and end apart: 3 -> 0, of which waited for: 2 -> 0; matrix products, arithmetic and copies ran while one was open for 29% -> 0% of each run, Pallas kernels for 0% -> 0%
where the time goes in v2:
time: 36.4 us; the launch traced here: 36.3 us
  Pallas kernels  35 us (96%)
  between operations  1.29 us (4%)
    pallas_call x1, Pallas kernels, body(): pl.pallas_call(functools.partial(kernel, n_blk), out_shape=(jax.ShapeDtyp...  33 us
    pallas_call x1, Pallas kernels, store_by_kernel(): pl.pallas_call(store_kernel, out_shape=(jax.ShapeDtypeStruct((series, ran...  2.03 us

profile of v2, /device:TPU:1, one launch (start us, length us, event | category | flops | bytes accessed | tf_op | source)
XLA Modules:
  0.0 36.3 jit_solution(16948892963981226701)
XLA Ops:
  1.3 33.0 %stratum_step.1 = (bf16[6144,256]{1,0:T(8,128)(2,1)S(1)}, f32[2,3,2,2,64,128]{5,4,3,2,1,0:T(8,128)S(1)}) custom-call(bf16[6144,256]{1,0:T(8,128)(2,1)} %obs_hbm.1, s32[32,6144]{1,0:T(8,128)} %bitcast.3, bf16[6144,256]{1,0:T(8,128)(2,1)} %fac_hbm.1, f32[1,256,256]{2,1,0:T(8,128)} %x_hbm.1, f32[1,256,256]{2,1,0:T(8,128)} %m_hbm.1, f32[1,256,256]{2,1,0:T(8,128)} %v_hbm.1, ...), custom_call_target="tpu_custom_call" | custom-call | tf_op jit(solution)/shard_map/stratum_step/pallas_call | solution.py:308
  34.3 2.0 %store_outputs.1 = (bf16[6144,256]{1,0:T(8,128)(2,1)}, f32[1,256,256]{2,1,0:T(8,128)}, f32[1,256,256]{2,1,0:T(8,128)}, f32[1,256,256]{2,1,0:T(8,128)}) custom-call(bf16[6144,256]{1,0:T(8,128)(2,1)S(1)} %get-tuple-element.6.fnew, f32[2,3,256,128]{3,2,1,0:T(8,128)S(1)} %bitcast.2), custom_call_target="tpu_custom_call" | custom-call | tf_op jit(solution)/shard_map/store_outputs/pallas_call | solution.py:370
